TPU v7x, 32 devices: a whole 2x2x4 slice. The times are simulated.
32 devices in a mesh: parts: 2 (over x), gy: 16 (over z, y, core).
Axes of the slice: x: 2, y: 2, z: 4, core: 2. Of those that a mesh axis runs over, the one named last changes fastest.
Arguments:
- zero_filled: float32 [32, 2, 64, 128], P(('parts', 'gy')), parts along dimension 0, may hold values from -6 to 6
- coil_maps: bfloat16 [32, 2, 32, 64, 128], P(('parts', 'gy')), parts along dimension 0, may hold values from -0.75 to 0.75
- offsets: int32 [128], P('parts'), parts along dimension 0, may hold values from 0 to 3
- step_sizes: float32 [1], replicated, may hold values from 0.6 to 1.4
- w_in: bfloat16 [64, 2, 3, 3], replicated, may hold values from -1.5 to 1.5
- b_in: float32 [64], replicated, may hold values from -0.5 to 0.5
- w_mid: bfloat16 [64, 64, 3, 3], replicated, may hold values from -0.25 to 0.25
- b_mid: float32 [64], replicated, may hold values from -0.5 to 0.5
- w_out: bfloat16 [2, 64, 3, 3], replicated, may hold values from -0.125 to 0.125
- b_out: float32 [2], replicated, may hold values from -0.5 to 0.5
Outputs:
- recon: float32 [32, 2, 64, 128], P(('parts', 'gy')), parts along dimension 0
There are 2 independent parts, one for each index of `parts`. A program takes and returns all parts, laid end to end along the dimension named above; an argument that names none is the same for every part. Nothing has to cross between parts.
Inputs may be any that keep to these rules, and one draw needn't show every extreme that they name: Readout row x samples the phase-encode lines offsets[x] + 4 m.
All inputs are finite; a program needn't handle non-finite values.
Results may differ from a plain program's by a relative error of at most 0.0012.
Values may be sent and summed in bfloat16 or wider, within the bound.
No kernel may reach another device: no remote copies, remote signals or barrier semaphores. Data moves between devices by JAX's collectives and lax.ppermute only.
A program may use at most 64 MiB of HBM per device.

v0:
```python
import jax
import jax.numpy as jnp
from jax import lax
from jax.sharding import PartitionSpec as P


def phase_tables(offsets):
    turns = jnp.arange(4, dtype=jnp.int32)[:, None] * offsets[None, :] % 4
    cosines = (turns == 0).astype(jnp.float32) - (turns == 2).astype(jnp.float32)
    sines = (turns == 3).astype(jnp.float32) - (turns == 1).astype(jnp.float32)
    return (cosines, sines)


def fold_normal(maps_list, field_list, cosines, sines):
    folded_real = None
    folded_imag = None
    for partner in range(4):
        maps_real = maps_list[partner][:, 0].astype(jnp.float32)
        maps_imag = maps_list[partner][:, 1].astype(jnp.float32)
        field_real = field_list[partner][:, 0][:, None]
        field_imag = field_list[partner][:, 1][:, None]
        coil_real = maps_real * field_real - maps_imag * field_imag
        coil_imag = maps_real * field_imag + maps_imag * field_real
        cosine = cosines[partner][None, None, :, None]
        sine = sines[partner][None, None, :, None]
        term_real = cosine * coil_real - sine * coil_imag
        term_imag = cosine * coil_imag + sine * coil_real
        if partner == 0:
            folded_real, folded_imag = (term_real, term_imag)
        else:
            folded_real = folded_real + term_real
            folded_imag = folded_imag + term_imag
    folded_real = 0.25 * folded_real
    folded_imag = 0.25 * folded_imag
    own_real = maps_list[0][:, 0].astype(jnp.float32)
    own_imag = maps_list[0][:, 1].astype(jnp.float32)
    normal_real = jnp.sum(own_real * folded_real + own_imag * folded_imag, axis=1)
    normal_imag = jnp.sum(own_real * folded_imag - own_imag * folded_real, axis=1)
    return jnp.stack([normal_real, normal_imag], axis=1)


def convolve(inputs, kernel):
    return lax.conv_general_dilated(
        inputs,
        kernel,
        (1, 1),
        "SAME",
        dimension_numbers=("NCHW", "OIHW", "NCHW"),
        preferred_element_type=jnp.float32,
    )


def denoise(stepped, w_in, b_in, w_mid, b_mid, w_out, b_out):
    stepped_low = stepped.astype(jnp.bfloat16)
    hidden_one = jax.nn.relu(convolve(stepped_low, w_in) + b_in[None, :, None, None]).astype(
        jnp.bfloat16
    )
    hidden_two = jax.nn.relu(convolve(hidden_one, w_mid) + b_mid[None, :, None, None]).astype(
        jnp.bfloat16
    )
    return stepped + convolve(hidden_two, w_out) + b_out[None, :, None, None]


def per_device(zero_filled, coil_maps, offsets, step_sizes, w_in, b_in, w_mid, b_mid, w_out, b_out):
    cosines, sines = phase_tables(offsets)
    devices = lax.axis_size("gy")
    field = zero_filled
    width_piece = zero_filled.shape[2] // devices
    first_row = lax.axis_index("gy") * width_piece
    cos_piece = lax.dynamic_slice_in_dim(cosines, first_row, width_piece, 1)
    sin_piece = lax.dynamic_slice_in_dim(sines, first_row, width_piece, 1)
    maps_whole = lax.all_to_all(coil_maps, "gy", split_axis=3, concat_axis=0, tiled=True)
    quarter = maps_whole.shape[0] // 4
    maps_list = [jnp.roll(maps_whole, -partner * quarter, axis=0) for partner in range(4)]
    whole = lax.all_to_all(field, "gy", split_axis=2, concat_axis=0, tiled=True)
    field_list = [jnp.roll(whole, -partner * quarter, axis=0) for partner in range(4)]
    normal_whole = fold_normal(maps_list, field_list, cos_piece, sin_piece)
    normal = lax.all_to_all(normal_whole, "gy", split_axis=0, concat_axis=2, tiled=True)
    stepped = field - step_sizes[0] * (normal - zero_filled)
    field = denoise(stepped, w_in, b_in, w_mid, b_mid, w_out, b_out)
    return field


def solution(mesh):
    in_specs = (
        P(("parts", "gy"), None, None, None),
        P(("parts", "gy"), None, None, None, None),
        P("parts"),
        P(),
        P(),
        P(),
        P(),
        P(),
        P(),
        P(),
    )
    out_specs = P(("parts", "gy"), None, None, None)
    return jax.shard_map(
        per_device, mesh=mesh, in_specs=in_specs, out_specs=out_specs, check_vma=False
    )
```

profile of v0, /device:TPU:0, one launch (start us, length us, event | category | flops | bytes accessed | tf_op | source)
XLA Modules:
  0.0 121.8 jit_solution(7083519290412785793)
XLA Ops:
  0.0 1.6 %copy.53 = f32[1,2,64,128]{3,1,0,2:T(2,128)} copy(f32[1,2,64,128]{3,2,1,0:T(8,128)} %param.10) | data formatting | bytes 131072 | tf_op args[0]
  1.6 7.4 %all-to-all-start.1 = ((f32[1,2,64,128]{3,1,0,2:T(2,128)}), f32[1,2,64,128]{3,1,0,2:T(2,128)S(1)}, u32[]{:S(2)}, u32[]{:S(2)}) async-start(f32[1,2,64,128]{3,1,0,2:T(2,128)} %copy.53), calls=%async_computation.1 | async-start | bytes 131072 | tf_op jit(solution)/shard_map/all_to_all | solution.py:75
  9.0 2.9 %copy.49 = bf16[1,2,32,64,128]{4,2,1,0,3:T(8,128)(2,1)} copy(bf16[1,2,32,64,128]{4,3,2,1,0:T(8,128)(2,1)} %param.11) | data formatting | bytes 2097152 | tf_op args[1]
  11.9 4.0 %all-to-all-done.1 = f32[1,2,64,128]{3,1,0,2:T(2,128)S(1)} async-done(((f32[1,2,64,128]{3,1,0,2:T(2,128)}), f32[1,2,64,128]{3,1,0,2:T(2,128)S(1)}, u32[]{:S(2)}, u32[]{:S(2)}) %all-to-all-start.1) | async-done | bytes 65568 | tf_op jit(solution)/shard_map/all_to_all | solution.py:75
  15.9 3.7 %all-to-all-start = ((bf16[1,2,32,64,128]{4,2,1,0,3:T(8,128)(2,1)}), bf16[1,2,32,64,128]{4,2,1,0,3:T(8,128)(2,1)S(1)}, u32[]{:S(2)}, u32[]{:S(2)}) async-start(bf16[1,2,32,64,128]{4,2,1,0,3:T(8,128)(2,1)} %copy.49), calls=%async_computation | async-start | bytes 2097152 | tf_op jit(solution)/shard_map/all_to_all | solution.py:72
  19.6 0.1 constant_dynamic-slice_fusion
  19.8 22.6 %all-to-all-done = bf16[1,2,32,64,128]{4,2,1,0,3:T(8,128)(2,1)S(1)} async-done(((bf16[1,2,32,64,128]{4,2,1,0,3:T(8,128)(2,1)}), bf16[1,2,32,64,128]{4,2,1,0,3:T(8,128)(2,1)S(1)}, u32[]{:S(2)}, u32[]{:S(2)}) %all-to-all-start) | async-done | bytes 1048608 | tf_op jit(solution)/shard_map/all_to_all | solution.py:72
  42.5 0.4 slice_bitcast_fusion
  42.9 0.1 slice_bitcast_fusion.3
  43.0 0.1 copy.69
  43.1 2.8 %fusion.37 = (f32[16,4,128]{2,1,0:T(4,128)S(1)}, f32[16,4,128]{2,1,0:T(4,128)S(1)}) fusion(bf16[16,2,32,4,128]{4,2,1,3,0:T(8,128)(2,1)S(1)} %bitcast.193, bf16[16,2,32,4,128]{4,2,3,1,0:T(8,128)(2,1)S(1)} %bitcast.194, f32[4]{0:T(128)S(1)} %get-tuple-element.38, f32[16,4,128]{2,1,0:T(4,128)S(1)} %get-tuple-element.32, ...), kind=kLoop, calls=%fused_computation.57 | loop fusion | flops 25149440 | bytes 4522112 | tf_op jit(solution)/shard_map/reduce_sum | solution.py:37
  45.9 0.6 pad_maximum_fusion.3
  46.5 6.8 %all-to-all-start.2 = ((f32[16,2,4,128]{3,2,1,0:T(4,128)}), f32[16,2,4,128]{3,2,1,0:T(4,128)S(1)}, u32[]{:S(2)}, u32[]{:S(2)}) async-start(f32[16,2,4,128]{3,2,1,0:T(4,128)} %pad_maximum_fusion.3), calls=%async_computation.2 | async-start | bytes 131072 | tf_op jit(solution)/shard_map/all_to_all | solution.py:78
  54.0 6.2 %all-to-all-done.2 = f32[16,2,4,128]{3,2,1,0:T(4,128)S(1)} async-done(((f32[16,2,4,128]{3,2,1,0:T(4,128)}), f32[16,2,4,128]{3,2,1,0:T(4,128)S(1)}, u32[]{:S(2)}, u32[]{:S(2)}) %all-to-all-start.2) | async-done | bytes 65568 | tf_op jit(solution)/shard_map/all_to_all | solution.py:78
  60.3 0.1 copy.65
  60.4 0.1 pad.clone
  60.5 0.6 copy.58
  61.1 0.1 slice.240
  61.3 3.7 %fusion.21 = bf16[64,1,8,17,64]{4,2,3,0,1:T(8,128)(2,1)S(1)} fusion(f32[64]{0:T(128)S(1)} %copy-done.6, pred[8,17]{0,1:T(8,128)(4,1)S(1)} %copy-done.8, bf16[64,2,3,3]{0,1,3,2:T(2,128)(2,1)S(1)} %copy-done.4, bf16[2,64,1,7,2]{3,0,4,1,2:T(2,128)(2,1)S(1)} %slice.240, bf16[2,64,1,8,17]{3,0,4,1,2:T(2,128)(2,1)S(1)} %copy.58), kind=kOutput, calls=%fused_computation.23 | convolution fusion | flops 22747136 | bytes 1155208 | tf_op jit(solution)/shard_map/conv_general_dilated | solution.py:43
  65.1 5.6 %fusion.23 = bf16[64,1,8,17,64]{4,2,3,0,1:T(8,128)(2,1)S(1)} fusion(f32[64]{0:T(128)S(1)} %copy-done.7, pred[8,17]{0,1:T(8,128)(4,1)S(1)} %copy-done.8, bf16[64,64,3,3]{1,0,3,2:T(8,128)(2,1)S(1)} %copy-done, bf16[64,1,7,1,64]{4,2,3,0,1:T(8,128)(2,1)S(1)} %get-tuple-element.10, bf16[64,1,7,1,64]{4,2,3,0,1:T(8,128)(2,1)S(1)} %get-tuple-element.9, ...), kind=kOutput, calls=%fused_computation.25 | convolution fusion | flops 643497984 | bytes 2417032 | tf_op jit(solution)/shard_map/conv_general_dilated | solution.py:43
  70.7 49.3 %fusion.18 = f32[64,8,17,2]{1,3,2,0:T(2,128)S(1)} fusion(bf16[2,64,3,3]{1,0,3,2:T(2,128)(2,1)S(1)} %copy-done.5, bf16[64,1,7,1,64]{4,2,3,0,1:T(8,128)(2,1)S(1)} %get-tuple-element.8, bf16[64,1,7,1,64]{4,2,3,0,1:T(8,128)(2,1)S(1)} %get-tuple-element.7, bf16[64,1,8,17,64]{4,2,3,0,1:T(8,128)(2,1)S(1)} %fusion.23), kind=kOutput, calls=%fused_computation.20 | convolution fusion | flops 26071040 | bytes 1300736 | tf_op jit(solution)/shard_map/conv_general_dilated | solution.py:43
  120.0 1.0 copy.59
  121.0 0.1 copy.64
  121.1 0.7 fusion.53
  (34 shorter events, 0.4 us)
Async XLA Ops:
  0.0 65.0 %copy-start = (bf16[64,64,3,3]{1,0,3,2:T(8,128)(2,1)S(1)}, bf16[64,64,3,3]{1,0,3,2:T(8,128)(2,1)}, u32[]{:S(2)}) copy-start(bf16[64,64,3,3]{1,0,3,2:T(8,128)(2,1)} %param.16) | copy-start | bytes 221188
  0.0 19.5 %copy-start.3 = (s32[64]{0:T(128)S(1)}, s32[64]{0:T(128)}, u32[]{:S(2)}) copy-start(s32[64]{0:T(128)} %param.12) | copy-start | bytes 772
  1.6 14.3 %all-to-all-start.1 = ((f32[1,2,64,128]{3,1,0,2:T(2,128)}), f32[1,2,64,128]{3,1,0,2:T(2,128)S(1)}, u32[]{:S(2)}, u32[]{:S(2)}) async-start(f32[1,2,64,128]{3,1,0,2:T(2,128)} %copy.53), calls=%async_computation.1 | async-start | bytes 131072 | tf_op jit(solution)/shard_map/all_to_all | solution.py:75
  15.9 26.6 %all-to-all-start = ((bf16[1,2,32,64,128]{4,2,1,0,3:T(8,128)(2,1)}), bf16[1,2,32,64,128]{4,2,1,0,3:T(8,128)(2,1)S(1)}, u32[]{:S(2)}, u32[]{:S(2)}) async-start(bf16[1,2,32,64,128]{4,2,1,0,3:T(8,128)(2,1)} %copy.49), calls=%async_computation | async-start | bytes 2097152 | tf_op jit(solution)/shard_map/all_to_all | solution.py:72
  43.1 17.2 %copy-start.1 = (f32[1,2,64,128]{3,2,1,0:T(8,128)S(1)}, f32[1,2,64,128]{3,2,1,0:T(8,128)}, u32[]{:S(2)}) copy-start(f32[1,2,64,128]{3,2,1,0:T(8,128)} %param.10) | copy-start | bytes 196612
  43.1 18.2 %copy-start.4 = (bf16[64,2,3,3]{0,1,3,2:T(2,128)(2,1)S(1)}, bf16[64,2,3,3]{0,1,3,2:T(2,128)(2,1)}, u32[]{:S(2)}) copy-start(bf16[64,2,3,3]{0,1,3,2:T(2,128)(2,1)} %param.14) | copy-start | bytes 6916
  43.1 18.2 %copy-start.6 = (f32[64]{0:T(128)S(1)}, f32[64]{0:T(128)}, u32[]{:S(2)}) copy-start(f32[64]{0:T(128)} %param.15) | copy-start | bytes 772
  43.1 18.2 %copy-start.8 = (pred[8,17]{0,1:T(8,128)(4,1)S(1)}, pred[8,17]{0,1:T(8,128)(4,1)}, u32[]{:S(2)}) copy-start(pred[8,17]{0,1:T(8,128)(4,1)} %constant.47) | copy-start | bytes 412
  46.5 13.7 %all-to-all-start.2 = ((f32[16,2,4,128]{3,2,1,0:T(4,128)}), f32[16,2,4,128]{3,2,1,0:T(4,128)S(1)}, u32[]{:S(2)}, u32[]{:S(2)}) async-start(f32[16,2,4,128]{3,2,1,0:T(4,128)} %pad_maximum_fusion.3), calls=%async_computation.2 | async-start | bytes 131072 | tf_op jit(solution)/shard_map/all_to_all | solution.py:78
  61.3 3.8 %copy-start.7 = (f32[64]{0:T(128)S(1)}, f32[64]{0:T(128)}, u32[]{:S(2)}) copy-start(f32[64]{0:T(128)} %param.17) | copy-start | bytes 772
  65.0 5.6 %copy-start.5 = (bf16[2,64,3,3]{1,0,3,2:T(2,128)(2,1)S(1)}, bf16[2,64,3,3]{1,0,3,2:T(2,128)(2,1)}, u32[]{:S(2)}) copy-start(bf16[2,64,3,3]{1,0,3,2:T(2,128)(2,1)} %param.18) | copy-start | bytes 6916
  70.7 50.4 %copy-start.2 = (f32[2]{0:T(128)S(1)}, f32[2]{0:T(128)}, u32[]{:S(2)}) copy-start(f32[2]{0:T(128)} %param.19) | copy-start | bytes 28
where the time goes:
time: 122 us
  matrix products  58.5 us (48%)
  waiting for transfers between devices  32.9 us (27%)
  starting transfers between devices  17.9 us (15%)
  local copies, waits for them, and re-layouts  7.39 us (6%)
  other arithmetic  4.21 us (3%)
    conv_general_dilated x3, matrix products, convolve(): lax.conv_general_dilated(inputs, kernel, (1, 1), 'SAME', dimension_number...  58.5 us
    all_to_all x1, waiting for transfers between devices, per_device(): lax.all_to_all(coil_maps, 'gy', split_axis=3, concat_axis=0, tiled=True)  22.6 us
    all_to_all x1, starting transfers between devices, per_device(): whole = lax.all_to_all(field, 'gy', split_axis=2, concat_axis=0, tiled=True)  7.39 us
    all_to_all x1, starting transfers between devices, per_device(): lax.all_to_all(normal_whole, 'gy', split_axis=0, concat_axis=2, tiled=True)  6.81 us
    all_to_all x1, waiting for transfers between devices, per_device(): lax.all_to_all(normal_whole, 'gy', split_axis=0, concat_axis=2, tiled=True)  6.25 us
    unnamed x22, local copies, waits for them, and re-layouts  4.72 us
    all_to_all x1, waiting for transfers between devices, per_device(): whole = lax.all_to_all(field, 'gy', split_axis=2, concat_axis=0, tiled=True)  4 us
    all_to_all x1, starting transfers between devices, per_device(): lax.all_to_all(coil_maps, 'gy', split_axis=3, concat_axis=0, tiled=True)  3.65 us
  transfers between devices with their start and end apart: 3, of which 3 were waited for; matrix products, arithmetic and copies ran while one was open for 3% of the time, Pallas kernels for 0%

commit v1 on v0

--- a/solution.py
+++ b/solution.py
@@ -69,7 +69,10 @@
     first_row = lax.axis_index("gy") * width_piece
     cos_piece = lax.dynamic_slice_in_dim(cosines, first_row, width_piece, 1)
     sin_piece = lax.dynamic_slice_in_dim(sines, first_row, width_piece, 1)
-    maps_whole = lax.all_to_all(coil_maps, "gy", split_axis=3, concat_axis=0, tiled=True)
+    maps_whole = jnp.concatenate(
+        lax.all_to_all(jnp.stack(jnp.split(coil_maps, lax.axis_size("gy"), axis=3)), "gy", 0, 0),
+        axis=0,
+    )
     quarter = maps_whole.shape[0] // 4
     maps_list = [jnp.roll(maps_whole, -partner * quarter, axis=0) for partner in range(4)]
     whole = lax.all_to_all(field, "gy", split_axis=2, concat_axis=0, tiled=True)

time: 122 us -> 131 us (1.074)
  local copies, waits for them, and re-layouts: 7.39 us -> 17.4 us
  waiting for transfers between devices: 32.9 us -> 28.9 us
  starting transfers between devices: 17.9 us -> 20.3 us
    unnamed x22 -> x36, local copies, waits for them, and re-layouts: 4.72 us -> 11.4 us
    all_to_all x1, waiting for transfers between devices: 4 us -> 0.01 us  [per_device(): whole = lax.all_to_all(field, 'gy', split_axis=2, concat_axis=0, tiled=True)]
    split x0 -> x1, local copies, waits for them, and re-layouts: none -> 2.44 us  [per_device(): jnp.split(coil_maps, lax.axis_size('gy'), axis=3)]
    all_to_all x1, starting transfers between devices: 3.65 us -> 6 us  [per_device(): lax.all_to_all(jnp.stack(jnp.split(coil_maps, lax.axis_size('gy'), axis=3...]
  transfers between devices with their start and end apart: 3 -> 3, of which waited for: 3 -> 2; matrix products, arithmetic and copies ran while one was open for 3% -> 10% of each run, Pallas kernels for 0% -> 0%
where the time goes in v1:
time: 131 us; the launch traced here: 130 us
  matrix products  58.5 us (45%)
  waiting for transfers between devices  28.9 us (22%)
  starting transfers between devices  20.3 us (15%)
  local copies, waits for them, and re-layouts  17.4 us (13%)
  other arithmetic  4.2 us (3%)
    conv_general_dilated x3, matrix products, convolve(): lax.conv_general_dilated(inputs, kernel, (1, 1), 'SAME', dimension_number...  58.5 us
    all_to_all x1, waiting for transfers between devices, per_device(): lax.all_to_all(jnp.stack(jnp.split(coil_maps, lax.axis_size('gy'), axis=3...  22.7 us
    unnamed x36, local copies, waits for them, and re-layouts  11.4 us
    all_to_all x1, starting transfers between devices, per_device(): whole = lax.all_to_all(field, 'gy', split_axis=2, concat_axis=0, tiled=True)  7.39 us
    all_to_all x1, starting transfers between devices, per_device(): lax.all_to_all(normal_whole, 'gy', split_axis=0, concat_axis=2, tiled=True)  6.86 us
    all_to_all x1, waiting for transfers between devices, per_device(): lax.all_to_all(normal_whole, 'gy', split_axis=0, concat_axis=2, tiled=True)  6.25 us
    all_to_all x1, starting transfers between devices, per_device(): lax.all_to_all(jnp.stack(jnp.split(coil_maps, lax.axis_size('gy'), axis=3...  6 us
    reduce_sum x1, other arithmetic, fold_normal(): jnp.sum(own_real * folded_real + own_imag * folded_imag, axis=1)  2.76 us
  transfers between devices with their start and end apart: 3, of which 2 were waited for; matrix products, arithmetic and copies ran while one was open for 10% of the time, Pallas kernels for 0%

profile of v1, /device:TPU:0, one launch (start us, length us, event | category | flops | bytes accessed | tf_op | source)
XLA Modules:
  0.0 130.3 jit_solution(12793959677542863951)
XLA Ops:
  0.0 1.6 %copy.113 = f32[1,2,64,128]{3,1,0,2:T(2,128)} copy(f32[1,2,64,128]{3,2,1,0:T(8,128)} %param.10) | data formatting | bytes 131072 | tf_op args[0]
  1.6 7.4 %all-to-all-start.1 = ((f32[1,2,64,128]{3,1,0,2:T(2,128)}), f32[1,2,64,128]{3,1,0,2:T(2,128)S(1)}, u32[]{:S(2)}, u32[]{:S(2)}) async-start(f32[1,2,64,128]{3,1,0,2:T(2,128)} %copy.113), calls=%async_computation.1 | async-start | bytes 131072 | tf_op jit(solution)/shard_map/all_to_all | solution.py:78
  9.0 2.4 %fusion.96 = (bf16[1,2,32,4,128]{4,3,2,1,0:T(4,128)(2,1)S(1)}, bf16[1,2,32,4,128]{4,3,2,1,0:T(4,128)(2,1)S(1)}, bf16[1,2,32,4,128]{4,3,2,1,0:T(4,128)(2,1)S(1)},...) fusion(bf16[1,2,32,64,128]{4,3,2,1,0:T(8,128)(2,1)} %param.11), kind=kLoop, calls=%fused_computation.188 | loop fusion | bytes 2097152 | tf_op jit(solution)/shard_map/split | solution.py:73
  11.4 0.6 fusion.68
  12.0 0.6 fusion.67
  12.7 0.6 fusion.66
  14.0 0.6 fusion.64
  14.6 0.6 fusion.63
  15.2 0.6 fusion.62
  15.9 0.6 fusion.61
  16.5 0.6 fusion.60
  17.2 0.6 fusion.59
  19.1 0.6 fusion.56
  21.6 6.0 %all-to-all-start = ((bf16[16,1,2,32,4,128]{5,3,4,2,1,0:T(8,128)(2,1)}), bf16[16,1,2,32,4,128]{5,3,4,2,1,0:T(8,128)(2,1)S(1)}, u32[]{:S(2)}, u32[]{:S(2)}) async-start(bf16[16,1,2,32,4,128]{5,3,4,2,1,0:T(8,128)(2,1)} %fusion.53), calls=%async_computation | async-start | bytes 2097152 | tf_op jit(solution)/shard_map/all_to_all | solution.py:73
  27.9 22.7 %all-to-all-done = bf16[16,1,2,32,4,128]{5,3,4,2,1,0:T(8,128)(2,1)S(1)} async-done(((bf16[16,1,2,32,4,128]{5,3,4,2,1,0:T(8,128)(2,1)}), bf16[16,1,2,32,4,128]{5,3,4,2,1,0:T(8,128)(2,1)S(1)}, u32[]{:S(2)}, u32[]{:S(2)}) %all-to-all-start) | async-done | bytes 1048608 | tf_op jit(solution)/shard_map/all_to_all | solution.py:73
  51.6 2.8 %fusion.37 = (f32[16,4,128]{2,1,0:T(4,128)S(1)}, f32[16,4,128]{2,1,0:T(4,128)S(1)}) fusion(bf16[16,2,32,4,128]{4,2,3,1,0:T(8,128)(2,1)S(1)} %bitcast.245, f32[4]{0:T(128)S(1)} %get-tuple-element.54, f32[16,4,128]{2,1,0:T(4,128)S(1)} %get-tuple-element.48, bf16[12,2,32,4,128]{4,2,3,0,1:T(8,128)(2,1)S(1)} %get-tuple-element.65, ...), kind=kLoop, calls=%fused_computation.57 | loop fusion | flops 25149440 | bytes 4522112 | tf_op jit(solution)/shard_map/reduce_sum | solution.py:37
  54.3 0.6 pad_maximum_fusion.3
  55.0 6.9 %all-to-all-start.2 = ((f32[16,2,4,128]{3,2,1,0:T(4,128)}), f32[16,2,4,128]{3,2,1,0:T(4,128)S(1)}, u32[]{:S(2)}, u32[]{:S(2)}) async-start(f32[16,2,4,128]{3,2,1,0:T(4,128)} %pad_maximum_fusion.3), calls=%async_computation.2 | async-start | bytes 131072 | tf_op jit(solution)/shard_map/all_to_all | solution.py:81
  62.5 6.2 %all-to-all-done.2 = f32[16,2,4,128]{3,2,1,0:T(4,128)S(1)} async-done(((f32[16,2,4,128]{3,2,1,0:T(4,128)}), f32[16,2,4,128]{3,2,1,0:T(4,128)S(1)}, u32[]{:S(2)}, u32[]{:S(2)}) %all-to-all-start.2) | async-done | bytes 65568 | tf_op jit(solution)/shard_map/all_to_all | solution.py:81
  69.8 3.7 %fusion.21 = bf16[64,1,8,17,64]{4,2,3,0,1:T(8,128)(2,1)S(1)} fusion(f32[64]{0:T(128)S(1)} %copy-done.6, pred[8,17]{0,1:T(8,128)(4,1)S(1)} %copy-done.8, bf16[64,2,3,3]{0,1,3,2:T(2,128)(2,1)S(1)} %copy-done.4, bf16[2,64,1,7,2]{3,0,4,1,2:T(2,128)(2,1)S(1)} %slice.240, bf16[2,64,1,8,17]{3,0,4,1,2:T(2,128)(2,1)S(1)} %copy.124), kind=kOutput, calls=%fused_computation.23 | convolution fusion | flops 22747136 | bytes 1155208 | tf_op jit(solution)/shard_map/conv_general_dilated | solution.py:43
  73.5 5.6 %fusion.23 = bf16[64,1,8,17,64]{4,2,3,0,1:T(8,128)(2,1)S(1)} fusion(f32[64]{0:T(128)S(1)} %copy-done.7, pred[8,17]{0,1:T(8,128)(4,1)S(1)} %copy-done.8, bf16[64,64,3,3]{1,0,3,2:T(8,128)(2,1)S(1)} %copy-done, bf16[64,1,7,1,64]{4,2,3,0,1:T(8,128)(2,1)S(1)} %get-tuple-element.10, bf16[64,1,7,1,64]{4,2,3,0,1:T(8,128)(2,1)S(1)} %get-tuple-element.9, ...), kind=kOutput, calls=%fused_computation.25 | convolution fusion | flops 643497984 | bytes 2417032 | tf_op jit(solution)/shard_map/conv_general_dilated | solution.py:43
  79.2 49.3 %fusion.18 = f32[64,8,17,2]{1,3,2,0:T(2,128)S(1)} fusion(bf16[2,64,3,3]{1,0,3,2:T(2,128)(2,1)S(1)} %copy-done.5, bf16[64,1,7,1,64]{4,2,3,0,1:T(8,128)(2,1)S(1)} %get-tuple-element.8, bf16[64,1,7,1,64]{4,2,3,0,1:T(8,128)(2,1)S(1)} %get-tuple-element.7, bf16[64,1,8,17,64]{4,2,3,0,1:T(8,128)(2,1)S(1)} %fusion.23), kind=kOutput, calls=%fused_computation.20 | convolution fusion | flops 26071040 | bytes 1300736 | tf_op jit(solution)/shard_map/conv_general_dilated | solution.py:43
  128.4 1.0 copy.125
  129.6 0.7 fusion.69
  (51 shorter events, 6.1 us)
Async XLA Ops:
  0.0 73.5 %copy-start = (bf16[64,64,3,3]{1,0,3,2:T(8,128)(2,1)S(1)}, bf16[64,64,3,3]{1,0,3,2:T(8,128)(2,1)}, u32[]{:S(2)}) copy-start(bf16[64,64,3,3]{1,0,3,2:T(8,128)(2,1)} %param.16) | copy-start | bytes 221188
  1.6 20.0 %all-to-all-start.1 = ((f32[1,2,64,128]{3,1,0,2:T(2,128)}), f32[1,2,64,128]{3,1,0,2:T(2,128)S(1)}, u32[]{:S(2)}, u32[]{:S(2)}) async-start(f32[1,2,64,128]{3,1,0,2:T(2,128)} %copy.113), calls=%async_computation.1 | async-start | bytes 131072 | tf_op jit(solution)/shard_map/all_to_all | solution.py:78
  11.4 16.2 %copy-start.3 = (s32[64]{0:T(128)S(1)}, s32[64]{0:T(128)}, u32[]{:S(2)}) copy-start(s32[64]{0:T(128)} %param.12) | copy-start | bytes 772
  21.6 29.0 %all-to-all-start = ((bf16[16,1,2,32,4,128]{5,3,4,2,1,0:T(8,128)(2,1)}), bf16[16,1,2,32,4,128]{5,3,4,2,1,0:T(8,128)(2,1)S(1)}, u32[]{:S(2)}, u32[]{:S(2)}) async-start(bf16[16,1,2,32,4,128]{5,3,4,2,1,0:T(8,128)(2,1)} %fusion.53), calls=%async_computation | async-start | bytes 2097152 | tf_op jit(solution)/shard_map/all_to_all | solution.py:73
  51.5 17.2 %copy-start.1 = (f32[1,2,64,128]{3,2,1,0:T(8,128)S(1)}, f32[1,2,64,128]{3,2,1,0:T(8,128)}, u32[]{:S(2)}) copy-start(f32[1,2,64,128]{3,2,1,0:T(8,128)} %param.10) | copy-start | bytes 196612
  51.5 18.2 %copy-start.4 = (bf16[64,2,3,3]{0,1,3,2:T(2,128)(2,1)S(1)}, bf16[64,2,3,3]{0,1,3,2:T(2,128)(2,1)}, u32[]{:S(2)}) copy-start(bf16[64,2,3,3]{0,1,3,2:T(2,128)(2,1)} %param.14) | copy-start | bytes 6916
  51.5 18.2 %copy-start.6 = (f32[64]{0:T(128)S(1)}, f32[64]{0:T(128)}, u32[]{:S(2)}) copy-start(f32[64]{0:T(128)} %param.15) | copy-start | bytes 772
  51.5 18.2 %copy-start.8 = (pred[8,17]{0,1:T(8,128)(4,1)S(1)}, pred[8,17]{0,1:T(8,128)(4,1)}, u32[]{:S(2)}) copy-start(pred[8,17]{0,1:T(8,128)(4,1)} %constant.47) | copy-start | bytes 412
  55.0 13.8 %all-to-all-start.2 = ((f32[16,2,4,128]{3,2,1,0:T(4,128)}), f32[16,2,4,128]{3,2,1,0:T(4,128)S(1)}, u32[]{:S(2)}, u32[]{:S(2)}) async-start(f32[16,2,4,128]{3,2,1,0:T(4,128)} %pad_maximum_fusion.3), calls=%async_computation.2 | async-start | bytes 131072 | tf_op jit(solution)/shard_map/all_to_all | solution.py:81
  69.8 3.8 %copy-start.7 = (f32[64]{0:T(128)S(1)}, f32[64]{0:T(128)}, u32[]{:S(2)}) copy-start(f32[64]{0:T(128)} %param.17) | copy-start | bytes 772
  73.5 5.6 %copy-start.5 = (bf16[2,64,3,3]{1,0,3,2:T(2,128)(2,1)S(1)}, bf16[2,64,3,3]{1,0,3,2:T(2,128)(2,1)}, u32[]{:S(2)}) copy-start(bf16[2,64,3,3]{1,0,3,2:T(2,128)(2,1)} %param.18) | copy-start | bytes 6916
  79.2 50.4 %copy-start.2 = (f32[2]{0:T(128)S(1)}, f32[2]{0:T(128)}, u32[]{:S(2)}) copy-start(f32[2]{0:T(128)} %param.19) | copy-start | bytes 28
